TPU v7x, 256 devices: a whole 4x4x8 slice. The times are simulated.
256 devices in a mesh: gx: 16 (over x, z_hi), gy: 4 (over z_lo, core), sa: 4 (over y).
Axes of the slice: x: 4, y: 4, z: 8 (z_hi: 4, z_lo: 2; z = z_hi * 2 + z_lo), core: 2. Of those that a mesh axis runs over, the one named last changes fastest.
Arguments:
- scalar_field: float32 [64, 1, 1024, 512], P('sa', None, 'gx', 'gy'), may hold values from -80 to 80, as said below
- start_basis: float32 [1024, 128], replicated, may hold values from -6 to 6
Outputs:
- core_tensor: float32 [64, 1, 128, 512], P(('sa', 'gx'), None, 'gy')
- leading_basis: float32 [1024, 128], P(('gx', 'gy', 'sa'))
Inputs may be any that keep to these rules, and one draw needn't show every extreme that they name: `scalar_field`: every entry is finite.
All inputs are finite; a program needn't handle non-finite values.
Results may differ from a plain program's by a relative error of at most 0.0003.
Values sent between devices are 32-bit elements; how exact they have to be, the bound alone decides.
A program may use at most 64 MiB of HBM per device.

v0:
```python
import jax
import jax.numpy as jnp
from jax import lax
from jax.sharding import PartitionSpec as P

NX = 1024
S = 64
ITERS = 3


HIGHEST_PREC = lax.Precision.HIGHEST


def orthonormal(mapped):
    inner_gram = jnp.dot(
        mapped.T, mapped, precision=HIGHEST_PREC, preferred_element_type=jnp.float32
    )
    factor = jnp.linalg.cholesky(inner_gram)
    return jax.scipy.linalg.solve_triangular(factor, mapped.T, lower=True).T


def on_device(scalar_field, start_basis):
    fibres = lax.all_to_all(scalar_field, "gx", split_axis=0, concat_axis=2, tiled=True)
    total_cols = fibres.shape[3] * lax.axis_size("gy") * S * fibres.shape[1]
    devices = lax.axis_size(("gx", "gy", "sa"))
    rows_dev = NX // devices
    my_index = lax.axis_index(("gx", "gy", "sa"))
    cur_basis = start_basis
    partial_value = jnp.einsum(
        "stxy,stzy->xz", fibres, fibres, precision=HIGHEST_PREC, preferred_element_type=jnp.float32
    )
    gram_matrix = lax.psum(partial_value, ("gx", "gy", "sa")) / total_cols
    for iteration in range(ITERS):
        mapped = jnp.dot(
            gram_matrix, cur_basis, precision=HIGHEST_PREC, preferred_element_type=jnp.float32
        )
        cur_basis = orthonormal(orthonormal(mapped))
    own_rows = lax.dynamic_slice_in_dim(cur_basis, my_index * rows_dev, rows_dev, 0)
    projected = jnp.einsum(
        "xk,stxy->stky",
        cur_basis,
        fibres,
        precision=HIGHEST_PREC,
        preferred_element_type=jnp.float32,
    )
    core_tensor = lax.all_to_all(projected, "gy", split_axis=2, concat_axis=3, tiled=True)
    return (core_tensor, own_rows)


def solution(mesh):
    placed = (P("sa", None, "gx", "gy"), P())
    return jax.shard_map(
        on_device,
        mesh=mesh,
        in_specs=placed,
        out_specs=(P(("sa", "gx"), None, "gy", None), P(("gx", "gy", "sa"), None)),
        check_vma=False,
    )
```

profile of v0, /device:TPU:1, one launch (start us, length us, event | category | flops | bytes accessed | tf_op | source)
XLA Modules:
  0.0 485.9 jit_solution(152987251267350413)
XLA Ops:
  7.2 28.0 %all_to_all.27 = f32[16,1,64,128]{3,2,1,0:T(8,128)S(1)} all-to-all(f32[16,1,64,128]{3,2,1,0:T(8,128)} %param.5), channel_id=1, replica_groups=mesh['gx'=16,'gy'=4,'sa'=4] {'gx'}, dimensions={0} | all-to-all | bytes 1048576 | tf_op jit(solution)/shard_map/all_to_all | solution.py:23
  35.2 5.0 %fusion.49 = f32[1024,1024]{1,0:T(8,128)} fusion(f32[1024,128]{1,0:T(8,128)S(1)} %bitcast.102), kind=kOutput, calls=%fused_computation.72 | convolution fusion | flops 1610612736 | bytes 4718592 | tf_op jit(solution)/shard_map/stxy,stzy->xz/dot_general | solution.py:29
  40.2 264.8 %all-reduce.2.cloned.1.call-done = f32[1024,1024]{1,0:T(8,128)} async-done(((f32[1024,1024]{1,0:T(8,128)}), f32[1024,1024]{1,0:T(8,128)}) %all-reduce.2.cloned.1.call-update) | async-done | bytes 4194320 | tf_op jit(solution)/shard_map/psum | solution.py:32
  305.0 5.4 %fusion.4 = f32[1024,128]{1,0:T(8,128)S(1)} fusion(f32[1024,128]{1,0:T(8,128)S(1)} %copy-done, f32[1024,1024]{1,0:T(8,128)} %all-reduce.2.cloned.1.call-done), kind=kOutput, calls=%fused_computation.4 | convolution fusion | flops 1611661312 | bytes 5242880 | tf_op jit(solution)/shard_map/dot_general | solution.py:34
  310.4 1.0 fusion.50
  311.5 11.7 %cholesky.104 = f32[128,128]{1,0:T(8,128)S(1)} custom-call(f32[128,128]{1,0:T(8,128)S(1)} %fusion.35), custom_call_target="Cholesky" | custom-call | tf_op jit(solution)/shard_map/jit(cholesky)/cholesky | solution.py:18
  323.9 0.7 fusion.15
  324.6 9.8 %custom-call.10 = f32[1,128,128]{1,2,0:T(8,128)S(1)} custom-call(f32[1,128,128]{2,1,0:T(8,128)S(1)} %fusion.15), custom_call_target="InvertDiagBlocksLowerTriangular" | custom-call | tf_op jit(solution)/shard_map/jit(_solve_triangular)/triangular_solve | solution.py:19
  335.8 11.7 %cholesky.115 = f32[128,128]{1,0:T(8,128)S(1)} custom-call(f32[128,128]{1,0:T(8,128)S(1)} %fusion.33), custom_call_target="Cholesky" | custom-call | tf_op jit(solution)/shard_map/jit(cholesky)/cholesky | solution.py:18
  348.5 0.7 fusion.16
  349.2 9.8 %custom-call.11 = f32[1,128,128]{1,2,0:T(8,128)S(1)} custom-call(f32[1,128,128]{2,1,0:T(8,128)S(1)} %fusion.16), custom_call_target="InvertDiagBlocksLowerTriangular" | custom-call | tf_op jit(solution)/shard_map/jit(_solve_triangular)/triangular_solve | solution.py:19
  359.6 5.2 %fusion.2 = f32[1024,128]{1,0:T(8,128)S(1)} fusion(f32[128,1024]{1,0:T(8,128)S(1)} %fusion.31, f32[1024,1024]{1,0:T(8,128)} %all-reduce.2.cloned.1.call-done), kind=kOutput, calls=%fused_computation.2 | convolution fusion | flops 1611661312 | bytes 5242880 | tf_op jit(solution)/shard_map/dot_general | solution.py:34
  364.9 1.0 fusion.52
  366.0 11.7 %cholesky.126 = f32[128,128]{1,0:T(8,128)S(1)} custom-call(f32[128,128]{1,0:T(8,128)S(1)} %fusion.30), custom_call_target="Cholesky" | custom-call | tf_op jit(solution)/shard_map/jit(cholesky)/cholesky | solution.py:18
  378.4 0.7 fusion.17
  379.1 9.8 %custom-call.12 = f32[1,128,128]{1,2,0:T(8,128)S(1)} custom-call(f32[1,128,128]{2,1,0:T(8,128)S(1)} %fusion.17), custom_call_target="InvertDiagBlocksLowerTriangular" | custom-call | tf_op jit(solution)/shard_map/jit(_solve_triangular)/triangular_solve | solution.py:19
  390.2 11.7 %cholesky.137 = f32[128,128]{1,0:T(8,128)S(1)} custom-call(f32[128,128]{1,0:T(8,128)S(1)} %fusion.28), custom_call_target="Cholesky" | custom-call | tf_op jit(solution)/shard_map/jit(cholesky)/cholesky | solution.py:18
  402.8 0.7 fusion.18
  403.4 9.8 %custom-call.13 = f32[1,128,128]{1,2,0:T(8,128)S(1)} custom-call(f32[1,128,128]{2,1,0:T(8,128)S(1)} %fusion.18), custom_call_target="InvertDiagBlocksLowerTriangular" | custom-call | tf_op jit(solution)/shard_map/jit(_solve_triangular)/triangular_solve | solution.py:19
  413.9 5.2 %fusion = f32[1024,128]{1,0:T(8,128)S(1)} fusion(f32[128,1024]{1,0:T(8,128)S(1)} %fusion.26, f32[1024,1024]{1,0:T(8,128)} %all-reduce.2.cloned.1.call-done), kind=kOutput, calls=%fused_computation | convolution fusion | flops 1611661312 | bytes 5242880 | tf_op jit(solution)/shard_map/dot_general | solution.py:34
  419.1 1.0 fusion.54
  420.2 11.7 %cholesky.148 = f32[128,128]{1,0:T(8,128)S(1)} custom-call(f32[128,128]{1,0:T(8,128)S(1)} %fusion.25), custom_call_target="Cholesky" | custom-call | tf_op jit(solution)/shard_map/jit(cholesky)/cholesky | solution.py:18
  432.6 0.7 fusion.19
  433.3 9.8 %custom-call.14 = f32[1,128,128]{1,2,0:T(8,128)S(1)} custom-call(f32[1,128,128]{2,1,0:T(8,128)S(1)} %fusion.19), custom_call_target="InvertDiagBlocksLowerTriangular" | custom-call | tf_op jit(solution)/shard_map/jit(_solve_triangular)/triangular_solve | solution.py:19
  443.1 0.6 fusion.9
  444.5 11.7 %cholesky.159 = f32[128,128]{1,0:T(8,128)S(1)} custom-call(f32[128,128]{1,0:T(8,128)S(1)} %fusion.23), custom_call_target="Cholesky" | custom-call | tf_op jit(solution)/shard_map/jit(cholesky)/cholesky | solution.py:18
  457.0 0.7 fusion.20
  457.7 9.8 %custom-call.15 = f32[1,128,128]{1,2,0:T(8,128)S(1)} custom-call(f32[1,128,128]{2,1,0:T(8,128)S(1)} %fusion.20), custom_call_target="InvertDiagBlocksLowerTriangular" | custom-call | tf_op jit(solution)/shard_map/jit(_solve_triangular)/triangular_solve | solution.py:19
  468.2 1.3 fusion.56
  469.4 5.5 %all-to-all-start.1 = ((f32[1,1,128,128]{3,1,0,2:T(1,128)}), f32[1,1,128,128]{3,1,0,2:T(1,128)S(1)}, u32[]{:S(2)}, u32[]{:S(2)}) async-start(f32[1,1,128,128]{3,1,0,2:T(1,128)} %bitcast.25), calls=%async_computation.1 | async-start | bytes 131072 | tf_op jit(solution)/shard_map/all_to_all | solution.py:46
  475.0 0.7 copy.20
  475.7 2.5 all-to-all-done.1
  (38 shorter events, 10.3 us)
Async XLA Ops:
  7.2 297.8 %copy-start = (f32[1024,128]{1,0:T(8,128)S(1)}, f32[1024,128]{1,0:T(8,128)}, u32[]{:S(2)}) copy-start(f32[1024,128]{1,0:T(8,128)} %param.6) | copy-start | bytes 1572868
  7.2 297.8 %all-reduce.2.cloned.1.call-start = ((), (), s32[]{:S(2)}) async-start(), calls=%async_computation.2 | async-start | bytes 8388608 | tf_op jit(solution)/shard_map/psum | solution.py:32
  469.4 8.7 %all-to-all-start.1 = ((f32[1,1,128,128]{3,1,0,2:T(1,128)}), f32[1,1,128,128]{3,1,0,2:T(1,128)S(1)}, u32[]{:S(2)}, u32[]{:S(2)}) async-start(f32[1,1,128,128]{3,1,0,2:T(1,128)} %bitcast.25), calls=%async_computation.1 | async-start | bytes 131072 | tf_op jit(solution)/shard_map/all_to_all | solution.py:46
Sparse Core Ops, SparseCore 0:
  40.3 264.6 all-reduce.1
where the time goes:
time: 490 us; the launch traced here: 486 us
  waiting for transfers between devices  267 us (54%)
  other arithmetic  137 us (28%)
  matrix products  30.6 us (6%)
  blocking collectives  28 us (6%)
  between operations  15.3 us (3%)
  starting transfers between devices  5.52 us (1%)
    psum x1, waiting for transfers between devices, on_device(): gram_matrix = lax.psum(partial_value, ('gx', 'gy', 'sa')) / total_cols  265 us
    another operation x18, other arithmetic, orthonormal(): factor = jnp.linalg.cholesky(inner_gram)  74.3 us
    another operation x12, other arithmetic, orthonormal(): return jax.scipy.linalg.solve_triangular(factor, mapped.T, lower=True).T  62.8 us
    all_to_all x1, blocking collectives, on_device(): lax.all_to_all(scalar_field, 'gx', split_axis=0, concat_axis=2, tiled=True)  28 us
    dot_general x3, matrix products, on_device(): jnp.dot(gram_matrix, cur_basis, precision=HIGHEST_PREC, preferred_element...  15.8 us
  transfers between devices with their start and end apart: 2, of which 2 were waited for; matrix products, arithmetic and copies ran while one was open for 0% of the time, Pallas kernels for 0%

commit v1 on v0

v1 whole, which is shorter than its diff:
```python
import functools

import jax
import jax.numpy as jnp
from jax import lax
from jax.experimental import pallas as pl
from jax.experimental.pallas import tpu as pltpu
from jax.sharding import PartitionSpec as P

NX = 1024
S = 64
ITERS = 3


HIGHEST_PREC = lax.Precision.HIGHEST


def row_of(v, p):
    return jnp.broadcast_to(v[p:p + 1, :], v.shape)

def lane_of(v, c):
    return jnp.broadcast_to(v[:, c:c + 1], v.shape)

def inverse_factor(a_ref, rank):
    sub = lax.broadcasted_iota(jnp.int32, (8, rank), 0)
    lane = lax.broadcasted_iota(jnp.int32, (8, rank), 1)
    panels = rank // 8
    for k in range(panels):
        base = 8 * k
        more = k + 1 < panels
        panel = a_ref[base:base + 8, :]
        cols = [lane_of(panel, base + c) for c in range(8)]
        inside = (lane >= base) & (lane < base + 8)
        panel = jnp.where(inside, jnp.where(lane - base == sub, 1.0, 0.0), panel)
        if more:
            nxt = a_ref[base + 8:base + 16, :]
            ncols = [lane_of(nxt, base + c) for c in range(8)]
            nxt = jnp.where(inside, 0.0, nxt)
        diag = jnp.zeros((8, rank), jnp.float32)
        for p in range(8):
            d = row_of(cols[p], p)
            r = 1.0 / d
            diag = jnp.where(sub == p, d, diag)
            f = jnp.where(sub > p, cols[p] * r, 0.0)
            prow = row_of(panel, p)
            if more:
                g = ncols[p] * r
                nxt = nxt - g * prow
            if p < 7:
                for c in range(p + 1, 8):
                    crow = row_of(cols[c], p)
                    cols[c] = cols[c] - f * crow
                    if more:
                        ncols[c] = ncols[c] - g * crow
                panel = panel - f * prow
        root = lax.rsqrt(diag)
        scaled = panel * root
        a_ref[base:base + 8, :] = jnp.where(lane < base + 8, scaled, 0.0)
        if more:
            a_ref[base + 8:base + 16, :] = nxt
        if k + 2 < panels:
            low = base + 16
            upper = jnp.where(lane >= low, scaled, 0.0)
            upd = lax.dot_general(upper, scaled, (((0,), (0,)), ((), ())), precision=HIGHEST_PREC,
                                  preferred_element_type=jnp.float32)
            rest = a_ref[low:, :]
            lanes = lax.broadcasted_iota(jnp.int32, rest.shape, 1)
            rest = jnp.where((lanes >= base) & (lanes < base + 8), 0.0, rest)
            a_ref[low:, :] = rest - upd[low:, :]

def iterate_body(iters, g_ref, q0_ref, q_ref, y_ref, a_ref):
    rows, rank = q0_ref.shape
    tile = 256
    q_ref[...] = q0_ref[...]

    @pl.loop(0, iters)
    def _(it):
        @pl.loop(0, rows // tile)
        def _(t):
            at = pl.ds(pl.multiple_of(t * tile, tile), tile)
            y_ref[at, :] = jnp.dot(g_ref[at, :], q_ref[...], precision=HIGHEST_PREC, preferred_element_type=jnp.float32)
        q_ref[...] = y_ref[...]

        @pl.loop(0, 2)
        def _(twice):
            y = q_ref[...]
            a_ref[...] = lax.dot_general(y, y, (((0,), (0,)), ((), ())), precision=HIGHEST_PREC,
                                         preferred_element_type=jnp.float32)
            inverse_factor(a_ref, rank)
            q_ref[...] = lax.dot_general(q_ref[...], a_ref[...], (((1,), (1,)), ((), ())), precision=HIGHEST_PREC,
                                         preferred_element_type=jnp.float32)

def iterate(gram, start, iters):
    rows, rank = start.shape
    return pl.pallas_call(
        functools.partial(iterate_body, iters),
        out_shape=jax.ShapeDtypeStruct((rows, rank), jnp.float32),
        in_specs=[pl.BlockSpec(memory_space=pltpu.VMEM)] * 2,
        out_specs=pl.BlockSpec(memory_space=pltpu.VMEM),
        scratch_shapes=[pltpu.VMEM((rows, rank), jnp.float32), pltpu.VMEM((rank, rank), jnp.float32)],
        compiler_params=pltpu.CompilerParams(vmem_limit_bytes=40 * 1024 * 1024),
        name="iterate",
    )(gram, start)


def on_device(scalar_field, start_basis):
    fibres = lax.all_to_all(scalar_field, "gx", split_axis=0, concat_axis=2, tiled=True)
    total_cols = fibres.shape[3] * lax.axis_size("gy") * S * fibres.shape[1]
    devices = lax.axis_size(("gx", "gy", "sa"))
    rows_dev = NX // devices
    my_index = lax.axis_index(("gx", "gy", "sa"))
    partial_value = jnp.einsum(
        "stxy,stzy->xz", fibres, fibres, precision=HIGHEST_PREC, preferred_element_type=jnp.float32
    )
    gram_matrix = lax.psum(partial_value, ("gx", "gy", "sa")) / total_cols
    cur_basis = iterate(gram_matrix, start_basis, ITERS)
    own_rows = lax.dynamic_slice_in_dim(cur_basis, my_index * rows_dev, rows_dev, 0)
    projected = jnp.einsum(
        "xk,stxy->stky",
        cur_basis,
        fibres,
        precision=HIGHEST_PREC,
        preferred_element_type=jnp.float32,
    )
    core_tensor = lax.all_to_all(projected, "gy", split_axis=2, concat_axis=3, tiled=True)
    return (core_tensor, own_rows)


def solution(mesh):
    placed = (P("sa", None, "gx", "gy"), P())
    return jax.shard_map(
        on_device,
        mesh=mesh,
        in_specs=placed,
        out_specs=(P(("sa", "gx"), None, "gy", None), P(("gx", "gy", "sa"), None)),
        check_vma=False,
    )
```

time: 490 us -> 373 us (0.76)
  other arithmetic: 137 us -> 3.02 us
  Pallas kernels: 0 us -> 47.3 us
  matrix products: 30.6 us -> 6.61 us
    another operation x30 -> x0, other arithmetic: 137 us -> none  [the longest x18 74.3 us: orthonormal(): factor = jnp.linalg.cholesky(inner_gram)]
    pallas_call x0 -> x1, Pallas kernels: none -> 47.3 us  [iterate(): pl.pallas_call(functools.partial(iterate_body, iters), out_shape=jax.Shap...]
    dot_general x9 -> x0, matrix products: 20.6 us -> none  [the longest x3 15.8 us: on_device(): jnp.dot(gram_matrix, cur_basis, precision=HIGHEST_PREC, preferred_element...]
where the time goes in v1:
time: 373 us
  waiting for transfers between devices  267 us (72%)
  Pallas kernels  47.3 us (13%)
  blocking collectives  27.9 us (7%)
  between operations  14.1 us (4%)
  matrix products  6.61 us (2%)
  starting transfers between devices  5.53 us (1%)
    psum x1, waiting for transfers between devices, on_device(): gram_matrix = lax.psum(partial_value, ('gx', 'gy', 'sa')) / total_cols  265 us
    pallas_call x1, Pallas kernels, iterate(): pl.pallas_call(functools.partial(iterate_body, iters), out_shape=jax.Shap...  47.3 us
    all_to_all x1, blocking collectives, on_device(): lax.all_to_all(scalar_field, 'gx', split_axis=0, concat_axis=2, tiled=True)  27.9 us
  transfers between devices with their start and end apart: 2, of which 2 were waited for; matrix products, arithmetic and copies ran while one was open for 0% of the time, Pallas kernels for 0%

profile of v1, /device:TPU:1, one launch (start us, length us, event | category | flops | bytes accessed | tf_op | source)
XLA Modules:
  0.0 373.0 jit_solution(11752613422163644890)
XLA Ops:
  7.2 0.0 all-reduce.2.cloned.1.call-start
  7.2 27.9 %all_to_all.27 = f32[16,1,64,128]{3,2,1,0:T(8,128)S(1)} all-to-all(f32[16,1,64,128]{3,2,1,0:T(8,128)} %param.2), channel_id=1, replica_groups=mesh['gx'=16,'gy'=4,'sa'=4] {'gx'}, dimensions={0} | all-to-all | bytes 1048576 | tf_op jit(solution)/shard_map/all_to_all | solution.py:107
  35.1 5.0 %fusion = f32[1024,1024]{1,0:T(8,128)} fusion(f32[1024,128]{1,0:T(8,128)S(1)} %bitcast.19), kind=kOutput, calls=%fused_computation.3 | convolution fusion | flops 1610612736 | bytes 4718592 | tf_op jit(solution)/shard_map/stxy,stzy->xz/dot_general | solution.py:112
  40.1 0.0 all-reduce.2.cloned.1.call-update
  40.1 0.0 copy-start
  40.1 264.7 %all-reduce.2.cloned.1.call-done = f32[1024,1024]{1,0:T(8,128)} async-done(((f32[1024,1024]{1,0:T(8,128)}), f32[1024,1024]{1,0:T(8,128)}) %all-reduce.2.cloned.1.call-update) | async-done | bytes 4194320 | tf_op jit(solution)/shard_map/psum | solution.py:115
  304.8 3.0 broadcast_multiply_fusion.g_ref
  307.8 0.0 copy-done
  307.9 47.3 %iterate.1 = f32[1024,128]{1,0:T(8,128)S(1)} custom-call(f32[1024,1024]{1,0:T(8,128)S(1)} %broadcast_multiply_fusion.g_ref, f32[1024,128]{1,0:T(8,128)S(1)} %copy-done), custom_call_target="tpu_custom_call" | custom-call | tf_op jit(solution)/shard_map/iterate/pallas_call | solution.py:95
  355.2 1.6 fusion.1
  356.8 5.5 %all-to-all-start.1 = ((f32[1,1,128,128]{3,1,0,2:T(1,128)}), f32[1,1,128,128]{3,1,0,2:T(1,128)S(1)}, u32[]{:S(2)}, u32[]{:S(2)}) async-start(f32[1,1,128,128]{3,1,0,2:T(1,128)} %bitcast.4), calls=%async_computation.1 | async-start | bytes 131072 | tf_op jit(solution)/shard_map/all_to_all | solution.py:125
  362.3 0.6 constant_dynamic-slice_fusion
  362.9 2.7 all-to-all-done.1
  365.5 0.6 copy.9
Async XLA Ops:
  7.2 297.7 %all-reduce.2.cloned.1.call-start = ((), (), s32[]{:S(2)}) async-start(), calls=%async_computation.2 | async-start | bytes 8388608 | tf_op jit(solution)/shard_map/psum | solution.py:115
  40.1 267.8 %copy-start = (f32[1024,128]{1,0:T(8,128)S(1)}, f32[1024,128]{1,0:T(8,128)}, u32[]{:S(2)}) copy-start(f32[1024,128]{1,0:T(8,128)} %q0_ref.1) | copy-start | bytes 1572868
  356.8 8.8 %all-to-all-start.1 = ((f32[1,1,128,128]{3,1,0,2:T(1,128)}), f32[1,1,128,128]{3,1,0,2:T(1,128)S(1)}, u32[]{:S(2)}, u32[]{:S(2)}) async-start(f32[1,1,128,128]{3,1,0,2:T(1,128)} %bitcast.4), calls=%async_computation.1 | async-start | bytes 131072 | tf_op jit(solution)/shard_map/all_to_all | solution.py:125
Sparse Core Ops, SparseCore 0:
  40.2 264.5 all-reduce.1

commit v2 on v1

--- a/solution.py
+++ b/solution.py
@@ -103,16 +103,186 @@
     )(gram, start)
 
 
+MESH = pl.DeviceIdType.MESH
+
+def place():
+    gx, gy, sa = lax.axis_index("gx"), lax.axis_index("gy"), lax.axis_index("sa")
+    return gx // 4, sa, (gx % 4) * 2 + gy // 2, gy % 2
+
+def device_at(x, y, z, core):
+    return {"gx": x * 4 + z // 2, "gy": (z % 2) * 2 + core, "sa": y}
+
+def gram_body(scale, f_ref, out_ref, cat, part, r0, r1, r2, r3, zout, zin, zall,
+              cat_sems, rs_send, rs_recv, zr_send, zr_recv, za_send, za_recv,
+              ag_send, ag_recv, core_send, core_recv):
+    x, y, z, core = place()
+    rbufs = (r0, r1, r2, r3)
+    mate = device_at(x, y, z, 1 - core)
+    pair = lambda i: i + 1 - 2 * (i % 2)
+    dims = (
+        (((x + 1) // 2) % 2, device_at(pair(x), y, z, core)),
+        (((y + 1) // 2) % 2, device_at(x, pair(y), z, core)),
+        (x // 2, device_at(3 - x, y, z, core)),
+        (y // 2, device_at(x, 3 - y, z, core)),
+    )
+    zpeers = [device_at(x, y, (z + o) % 8, core) for o in range(1, 8)]
+
+    barrier = pltpu.get_barrier_semaphore()
+    peers = [mate] + [d[1] for d in dims] + zpeers
+    for peer in peers:
+        pl.semaphore_signal(barrier, inc=1, device_id=peer, device_id_type=MESH)
+    pl.semaphore_wait(barrier, len(peers))
+
+    def remote(src, dst, ss, rs, dev):
+        return pltpu.make_async_remote_copy(src_ref=src, dst_ref=dst, send_sem=ss, recv_sem=rs,
+                                            device_id=dev, device_id_type=MESH)
+    swap = remote(f_ref, cat.at[:, pl.ds(128, 128)], cat_sems.at[0], cat_sems.at[1], mate)
+    swap.start()
+    cat[:, 0:128] = f_ref[...]
+    swap.wait()
+
+    sent = []
+    offs = []
+    for q in range(4):
+        o = [0]
+        for s in range(4):
+            bit = dims[(q + s) % 4][0]
+            o.append(o[-1] + bit * (64 >> s))
+        offs.append(o)
+
+    def halve(q, s):
+        half = 64 >> s
+        bit, dev = dims[(q + s) % 4]
+        row = pl.multiple_of(offs[q][s] + (1 - bit) * half, 8)
+        return remote(part.at[q, pl.ds(row, half), :], rbufs[s].at[q],
+                      rs_send.at[s, q], rs_recv.at[s, q], dev)
+
+    top = core * 512
+    for q in range(4):
+        lhs = cat[pl.ds(pl.multiple_of(top + q * 128, 128), 128), :]
+        part[q] = lax.dot_general(lhs, cat[...], (((1,), (1,)), ((), ())), precision=HIGHEST_PREC,
+                                  preferred_element_type=jnp.float32)
+        c = halve(q, 0)
+        c.start()
+        sent.append(c)
+    for s in range(4):
+        half = 64 >> s
+        for q in range(4):
+            halve(q, s).wait_recv()
+            keep = pl.ds(pl.multiple_of(offs[q][s + 1], 8), half)
+            part[q, keep, :] = part[q, keep, :] + rbufs[s][q]
+            if s < 3:
+                c = halve(q, s + 1)
+                c.start()
+                sent.append(c)
+    for q in range(4):
+        rows = pl.ds(pl.multiple_of(offs[q][4], 8), 8)
+        for t in range(8):
+            zout[t, q] = part[q, rows, 128 * t:128 * t + 128]
+    def zscatter(o):
+        return remote(zout.at[(z + o) % 8], zin.at[o - 1], zr_send.at[o - 1], zr_recv.at[o - 1], zpeers[o - 1])
+    def zgather(o):
+        return remote(zall.at[0], zall.at[o], za_send.at[o - 1], za_recv.at[o - 1], zpeers[o - 1])
+    for o in range(1, 8):
+        c = zscatter(o)
+        c.start()
+        sent.append(c)
+    total = zout[z]
+    for o in range(1, 8):
+        zscatter(o).wait_recv()
+        total = total + zin[o - 1]
+    zall[0] = total * scale
+    for o in range(1, 8):
+        c = zgather(o)
+        c.start()
+        sent.append(c)
+
+    def at_row(q, row, size):
+        return pl.ds(pl.multiple_of(top + q * 128 + row, 8), size)
+
+    for o in range(8):
+        if o:
+            zgather(o).wait_recv()
+        lanes = pl.ds(pl.multiple_of(((z + 8 - o) % 8) * 128, 128), 128)
+        for q in range(4):
+            out_ref[at_row(q, offs[q][4], 8), lanes] = zall[o, q]
+
+    def grow(q, s):
+        ref = out_ref.at[at_row(q, offs[q][s + 1], 64 >> s), :]
+        return remote(ref, ref, ag_send.at[s, q], ag_recv.at[s, q], dims[(q + s) % 4][1])
+
+    def hand(q, s):
+        if s == 4:
+            rows = at_row(q, offs[q][4], 8)
+        else:
+            half = 64 >> s
+            rows = at_row(q, offs[q][s] + (1 - dims[(q + s) % 4][0]) * half, half)
+        ref = out_ref.at[rows, :]
+        return remote(ref, ref, core_send.at[s, q], core_recv.at[s, q], mate)
+
+    def take(q, s):
+        if s == 4:
+            row, size = offs[q][4], 8
+        else:
+            size = 64 >> s
+            row = offs[q][s] + (1 - dims[(q + s) % 4][0]) * size
+        ref = out_ref.at[pl.ds(pl.multiple_of(512 - top + q * 128 + row, 8), size), :]
+        return remote(ref, ref, core_send.at[s, q], core_recv.at[s, q], mate)
+
+    for s in (3, 2, 1, 0):
+        for q in range(4):
+            if s < 3:
+                grown = offs[q][s + 1] + (1 - dims[(q + s + 1) % 4][0]) * (64 >> (s + 1))
+                ref = out_ref.at[at_row(q, grown, 64 >> (s + 1)), :]
+                remote(ref, ref, ag_send.at[s + 1, q], ag_recv.at[s + 1, q], mate).wait_recv()
+            c = grow(q, s)
+            c.start()
+            sent.append(c)
+            c = hand(q, s + 1)
+            c.start()
+            sent.append(c)
+    for q in range(4):
+        grown = offs[q][0] + (1 - dims[q % 4][0]) * 64
+        ref = out_ref.at[at_row(q, grown, 64), :]
+        remote(ref, ref, ag_send.at[0, q], ag_recv.at[0, q], mate).wait_recv()
+        c = hand(q, 0)
+        c.start()
+        sent.append(c)
+    for s in (4, 3, 2, 1, 0):
+        for q in range(4):
+            take(q, s).wait_recv()
+    for c in sent:
+        c.wait_send()
+
+def summed_gram(fibre, scale):
+    nx, width = fibre.shape
+    dma = lambda *shape: pltpu.SemaphoreType.DMA(shape)
+    vm = lambda *shape: pltpu.VMEM(shape, jnp.float32)
+    return pl.pallas_call(
+        functools.partial(gram_body, scale),
+        out_shape=jax.ShapeDtypeStruct((nx, nx), jnp.float32),
+        in_specs=[pl.BlockSpec(memory_space=pltpu.VMEM)],
+        out_specs=pl.BlockSpec(memory_space=pltpu.VMEM),
+        scratch_shapes=[
+            vm(nx, 2 * width), vm(4, 128, nx),
+            vm(4, 64, nx), vm(4, 32, nx), vm(4, 16, nx), vm(4, 8, nx),
+            vm(8, 4, 8, 128), vm(7, 4, 8, 128), vm(8, 4, 8, 128),
+            dma(2), dma(4, 4), dma(4, 4), dma(7), dma(7), dma(7), dma(7),
+            dma(4, 4), dma(4, 4), dma(5, 4), dma(5, 4),
+        ],
+        compiler_params=pltpu.CompilerParams(collective_id=0, has_side_effects=True,
+                                             vmem_limit_bytes=40 * 1024 * 1024),
+        name="summed_gram",
+    )(fibre)
+
+
 def on_device(scalar_field, start_basis):
     fibres = lax.all_to_all(scalar_field, "gx", split_axis=0, concat_axis=2, tiled=True)
     total_cols = fibres.shape[3] * lax.axis_size("gy") * S * fibres.shape[1]
     devices = lax.axis_size(("gx", "gy", "sa"))
     rows_dev = NX // devices
     my_index = lax.axis_index(("gx", "gy", "sa"))
-    partial_value = jnp.einsum(
-        "stxy,stzy->xz", fibres, fibres, precision=HIGHEST_PREC, preferred_element_type=jnp.float32
-    )
-    gram_matrix = lax.psum(partial_value, ("gx", "gy", "sa")) / total_cols
+    gram_matrix = summed_gram(fibres.reshape(NX, fibres.shape[3]), 1.0 / total_cols)
     cur_basis = iterate(gram_matrix, start_basis, ITERS)
     own_rows = lax.dynamic_slice_in_dim(cur_basis, my_index * rows_dev, rows_dev, 0)
     projected = jnp.einsum(

time: 373 us -> 149 us (0.40)
  waiting for transfers between devices: 267 us -> 18.9 us
  Pallas kernels: 47.3 us -> 111 us
  blocking collectives: 27.9 us -> 0 us
  between operations: 14.1 us -> 0.68 us
  starting transfers between devices: 5.53 us -> 15 us
  matrix products: 6.61 us -> 1.63 us
    psum x1 -> x0, waiting for transfers between devices: 265 us -> none  [on_device(): gram_matrix = lax.psum(partial_value, ('gx', 'gy', 'sa')) / total_cols]
    pallas_call x0 -> x1, Pallas kernels: none -> 63.7 us  [summed_gram(): pl.pallas_call(functools.partial(gram_body, scale), out_shape=jax.ShapeDt...]
    all_to_all x1 -> x0, blocking collectives: 27.9 us -> none  [on_device(): lax.all_to_all(scalar_field, 'gx', split_axis=0, concat_axis=2, tiled=True)]
    all_to_all x0 -> x1, waiting for transfers between devices: none -> 16.3 us  [on_device(): lax.all_to_all(scalar_field, 'gx', split_axis=0, concat_axis=2, tiled=True)]
    all_to_all x0 -> x1, starting transfers between devices: none -> 11.7 us  [on_device(): lax.all_to_all(scalar_field, 'gx', split_axis=0, concat_axis=2, tiled=True)]
    dot_general x1 -> x0, matrix products: 4.98 us -> none  [on_device(): jnp.einsum('stxy,stzy->xz', fibres, fibres, precision=HIGHEST_PREC, prefe...]
where the time goes in v2:
time: 149 us; the launch traced here: 148 us
  Pallas kernels  111 us (74%)
  waiting for transfers between devices  18.9 us (13%)
  starting transfers between devices  15 us (10%)
  matrix products  1.63 us (1%)
    pallas_call x1, Pallas kernels, summed_gram(): pl.pallas_call(functools.partial(gram_body, scale), out_shape=jax.ShapeDt...  63.7 us
    pallas_call x1, Pallas kernels, iterate(): pl.pallas_call(functools.partial(iterate_body, iters), out_shape=jax.Shap...  47.3 us
    all_to_all x1, waiting for transfers between devices, on_device(): lax.all_to_all(scalar_field, 'gx', split_axis=0, concat_axis=2, tiled=True)  16.3 us
    all_to_all x1, starting transfers between devices, on_device(): lax.all_to_all(scalar_field, 'gx', split_axis=0, concat_axis=2, tiled=True)  11.7 us
    all_to_all x1, starting transfers between devices, on_device(): lax.all_to_all(projected, 'gy', split_axis=2, concat_axis=3, tiled=True)  3.29 us
  transfers between devices with their start and end apart: 2, of which 2 were waited for; matrix products, arithmetic and copies ran while one was open for 0% of the time, Pallas kernels for 0%

profile of v2, /device:TPU:1, one launch (start us, length us, event | category | flops | bytes accessed | tf_op | source)
XLA Modules:
  0.0 148.5 jit_solution(6469109736006093540)
XLA Ops:
  0.6 0.0 copy-start
  0.6 11.7 %all-to-all-start = ((f32[16,1,64,128]{3,2,1,0:T(8,128)}), f32[16,1,64,128]{3,2,1,0:T(8,128)S(1)}, u32[]{:S(2)}, u32[]{:S(2)}) async-start(f32[16,1,64,128]{3,2,1,0:T(8,128)} %param.2), calls=%async_computation | async-start | bytes 1048576 | tf_op jit(solution)/shard_map/all_to_all | solution.py:280
  12.4 16.3 %all-to-all-done = f32[16,1,64,128]{3,2,1,0:T(8,128)S(1)} async-done(((f32[16,1,64,128]{3,2,1,0:T(8,128)}), f32[16,1,64,128]{3,2,1,0:T(8,128)S(1)}, u32[]{:S(2)}, u32[]{:S(2)}) %all-to-all-start) | async-done | bytes 524320 | tf_op jit(solution)/shard_map/all_to_all | solution.py:280
  28.6 63.7 %summed_gram.1.g_ref = f32[1024,1024]{1,0:T(8,128)S(1)} custom-call(f32[1024,128]{1,0:T(8,128)S(1)} %bitcast.17), custom_call_target="tpu_custom_call" | custom-call | tf_op jit(solution)/shard_map/summed_gram/pallas_call | solution.py:261
  92.4 0.0 copy-done
  92.4 47.3 %iterate.1 = f32[1024,128]{1,0:T(8,128)S(1)} custom-call(f32[1024,1024]{1,0:T(8,128)S(1)} %summed_gram.1.g_ref, f32[1024,128]{1,0:T(8,128)S(1)} %copy-done), custom_call_target="tpu_custom_call" | custom-call | tf_op jit(solution)/shard_map/iterate/pallas_call | solution.py:95
  139.7 1.6 %fusion = f32[128,128]{1,0:T(8,128)} fusion(f32[1024,128]{1,0:T(8,128)S(1)} %iterate.1, f32[1024,128]{1,0:T(8,128)S(1)} %bitcast.18), kind=kOutput, calls=%fused_computation.2 | convolution fusion | flops 201326592 | bytes 1114112 | tf_op jit(solution)/shard_map/xk,stxy->stky/dot_general | solution.py:288
  141.3 3.3 %all-to-all-start.1 = ((f32[1,1,128,128]{3,1,0,2:T(1,128)}), f32[1,1,128,128]{3,1,0,2:T(1,128)S(1)}, u32[]{:S(2)}, u32[]{:S(2)}) async-start(f32[1,1,128,128]{3,1,0,2:T(1,128)} %bitcast.4), calls=%async_computation.1 | async-start | bytes 131072 | tf_op jit(solution)/shard_map/all_to_all | solution.py:295
  144.6 0.6 constant_dynamic-slice_fusion
  145.2 2.7 %all-to-all-done.1 = f32[1,1,128,128]{3,1,0,2:T(1,128)S(1)} async-done(((f32[1,1,128,128]{3,1,0,2:T(1,128)}), f32[1,1,128,128]{3,1,0,2:T(1,128)S(1)}, u32[]{:S(2)}, u32[]{:S(2)}) %all-to-all-start.1) | async-done | bytes 65568 | tf_op jit(solution)/shard_map/all_to_all | solution.py:295
  147.9 0.6 copy.9
Async XLA Ops:
  0.6 91.7 %copy-start = (f32[1024,128]{1,0:T(8,128)S(1)}, f32[1024,128]{1,0:T(8,128)}, u32[]{:S(2)}) copy-start(f32[1024,128]{1,0:T(8,128)} %q0_ref.1) | copy-start | bytes 1572868
  0.6 28.0 %all-to-all-start = ((f32[16,1,64,128]{3,2,1,0:T(8,128)}), f32[16,1,64,128]{3,2,1,0:T(8,128)S(1)}, u32[]{:S(2)}, u32[]{:S(2)}) async-start(f32[16,1,64,128]{3,2,1,0:T(8,128)} %param.2), calls=%async_computation | async-start | bytes 1048576 | tf_op jit(solution)/shard_map/all_to_all | solution.py:280
  141.3 6.5 %all-to-all-start.1 = ((f32[1,1,128,128]{3,1,0,2:T(1,128)}), f32[1,1,128,128]{3,1,0,2:T(1,128)S(1)}, u32[]{:S(2)}, u32[]{:S(2)}) async-start(f32[1,1,128,128]{3,1,0,2:T(1,128)} %bitcast.4), calls=%async_computation.1 | async-start | bytes 131072 | tf_op jit(solution)/shard_map/all_to_all | solution.py:295

commit v3 on v2

--- a/solution.py
+++ b/solution.py
@@ -11,8 +11,15 @@
 S = 64
 ITERS = 3
 
-
-HIGHEST_PREC = lax.Precision.HIGHEST
+HI = lax.Precision.HIGHEST
+MESH = pl.DeviceIdType.MESH
+
+def place():
+    gx, gy, sa = lax.axis_index("gx"), lax.axis_index("gy"), lax.axis_index("sa")
+    return gx // 4, sa, (gx % 4) * 2 + gy // 2, gy % 2
+
+def device_at(x, y, z, core):
+    return {"gx": x * 4 + z // 2, "gy": (z % 2) * 2 + core, "sa": y}
 
 
 def row_of(v, p):
@@ -61,60 +68,28 @@
         if k + 2 < panels:
             low = base + 16
             upper = jnp.where(lane >= low, scaled, 0.0)
-            upd = lax.dot_general(upper, scaled, (((0,), (0,)), ((), ())), precision=HIGHEST_PREC,
+            upd = lax.dot_general(upper, scaled, (((0,), (0,)), ((), ())), precision=HI,
                                   preferred_element_type=jnp.float32)
             rest = a_ref[low:, :]
             lanes = lax.broadcasted_iota(jnp.int32, rest.shape, 1)
             rest = jnp.where((lanes >= base) & (lanes < base + 8), 0.0, rest)
             a_ref[low:, :] = rest - upd[low:, :]
 
-def iterate_body(iters, g_ref, q0_ref, q_ref, y_ref, a_ref):
-    rows, rank = q0_ref.shape
-    tile = 256
-    q_ref[...] = q0_ref[...]
-
-    @pl.loop(0, iters)
-    def _(it):
-        @pl.loop(0, rows // tile)
-        def _(t):
-            at = pl.ds(pl.multiple_of(t * tile, tile), tile)
-            y_ref[at, :] = jnp.dot(g_ref[at, :], q_ref[...], precision=HIGHEST_PREC, preferred_element_type=jnp.float32)
-        q_ref[...] = y_ref[...]
-
-        @pl.loop(0, 2)
-        def _(twice):
-            y = q_ref[...]
-            a_ref[...] = lax.dot_general(y, y, (((0,), (0,)), ((), ())), precision=HIGHEST_PREC,
-                                         preferred_element_type=jnp.float32)
-            inverse_factor(a_ref, rank)
-            q_ref[...] = lax.dot_general(q_ref[...], a_ref[...], (((1,), (1,)), ((), ())), precision=HIGHEST_PREC,
-                                         preferred_element_type=jnp.float32)
-
-def iterate(gram, start, iters):
-    rows, rank = start.shape
-    return pl.pallas_call(
-        functools.partial(iterate_body, iters),
-        out_shape=jax.ShapeDtypeStruct((rows, rank), jnp.float32),
-        in_specs=[pl.BlockSpec(memory_space=pltpu.VMEM)] * 2,
-        out_specs=pl.BlockSpec(memory_space=pltpu.VMEM),
-        scratch_shapes=[pltpu.VMEM((rows, rank), jnp.float32), pltpu.VMEM((rank, rank), jnp.float32)],
-        compiler_params=pltpu.CompilerParams(vmem_limit_bytes=40 * 1024 * 1024),
-        name="iterate",
-    )(gram, start)
-
-
-MESH = pl.DeviceIdType.MESH
-
-def place():
-    gx, gy, sa = lax.axis_index("gx"), lax.axis_index("gy"), lax.axis_index("sa")
-    return gx // 4, sa, (gx % 4) * 2 + gy // 2, gy % 2
-
-def device_at(x, y, z, core):
-    return {"gx": x * 4 + z // 2, "gy": (z % 2) * 2 + core, "sa": y}
-
-def gram_body(scale, f_ref, out_ref, cat, part, r0, r1, r2, r3, zout, zin, zall,
-              cat_sems, rs_send, rs_recv, zr_send, zr_recv, za_send, za_recv,
-              ag_send, ag_recv, core_send, core_recv):
+
+def split(v):
+    high = v.astype(jnp.bfloat16)
+    return high, (v - high.astype(jnp.float32)).astype(jnp.bfloat16)
+
+
+def dot3(a, b, contract):
+    one = lambda u, v: lax.dot_general(u, v, (contract, ((), ())), preferred_element_type=jnp.float32)
+    return one(a[0], b[0]) + (one(a[0], b[1]) + one(a[1], b[0]))
+
+
+def whole_body(scale, iters, field_ref, q0_ref, core_ref, rows_ref, own, other, high, low, part, r0, r1, r2, r3,
+               zout, zin, zall, out_ref, q_ref, y_ref, a_ref, proj,
+               fs_send, fs_recv, fw_send, fw_recv, rs_send, rs_recv, zr_send, zr_recv, za_send, za_recv,
+               ag_send, ag_recv, core_send, core_recv, last_sems):
     x, y, z, core = place()
     rbufs = (r0, r1, r2, r3)
     mate = device_at(x, y, z, 1 - core)
@@ -128,7 +103,9 @@
     zpeers = [device_at(x, y, (z + o) % 8, core) for o in range(1, 8)]
 
     barrier = pltpu.get_barrier_semaphore()
-    peers = [mate] + [d[1] for d in dims] + zpeers
+    gx, gy, sa = lax.axis_index("gx"), lax.axis_index("gy"), lax.axis_index("sa")
+    xpeers = [{"gx": (gx + o) % 16, "gy": gy, "sa": sa} for o in range(1, 16)]
+    peers = [mate, dims[1][1], dims[3][1]] + zpeers[0::2] + xpeers
     for peer in peers:
         pl.semaphore_signal(barrier, inc=1, device_id=peer, device_id_type=MESH)
     pl.semaphore_wait(barrier, len(peers))
@@ -136,12 +113,43 @@
     def remote(src, dst, ss, rs, dev):
         return pltpu.make_async_remote_copy(src_ref=src, dst_ref=dst, send_sem=ss, recv_sem=rs,
                                             device_id=dev, device_id_type=MESH)
-    swap = remote(f_ref, cat.at[:, pl.ds(128, 128)], cat_sems.at[0], cat_sems.at[1], mate)
-    swap.start()
-    cat[:, 0:128] = f_ref[...]
-    swap.wait()
-
     sent = []
+
+    def spread(o):
+        return remote(field_ref.at[(gx + o) % 16], own.at[gx], fs_send.at[o - 1], fs_recv.at[o - 1], xpeers[o - 1])
+
+    def forward(o):
+        block = (gx + 16 - o) % 16
+        src = own.at[block] if o else field_ref.at[block]
+        return remote(src, other.at[block], fw_send.at[o], fw_recv.at[o], mate)
+
+    order = (8, 4, 12, 6, 10, 7, 9, 5, 11, 2, 14, 3, 13, 1, 15)
+    for o in order:
+        c = spread(o)
+        c.start()
+        sent.append(c)
+    c = forward(0)
+    c.start()
+    sent.append(c)
+
+    def store(block, values, lanes):
+        rows = pl.ds(pl.multiple_of(block * 64, 64), 64)
+        high[rows, lanes], low[rows, lanes] = split(values)
+
+    mine, its = slice(0, 128), slice(128, 256)
+    store(gx, field_ref[gx], mine)
+    for o in reversed(order):
+        block = (gx + 16 - o) % 16
+        spread(o).wait_recv()
+        c = forward(o)
+        c.start()
+        sent.append(c)
+        store(block, own[block], mine)
+    for o in (0,) + order[::-1]:
+        block = (gx + 16 - o) % 16
+        remote(field_ref.at[0], other.at[block], fw_send.at[o], fw_recv.at[o], mate).wait_recv()
+        store(block, other[block], its)
+
     offs = []
     for q in range(4):
         o = [0]
@@ -159,9 +167,8 @@
 
     top = core * 512
     for q in range(4):
-        lhs = cat[pl.ds(pl.multiple_of(top + q * 128, 128), 128), :]
-        part[q] = lax.dot_general(lhs, cat[...], (((1,), (1,)), ((), ())), precision=HIGHEST_PREC,
-                                  preferred_element_type=jnp.float32)
+        rows = pl.ds(pl.multiple_of(top + q * 128, 128), 128)
+        part[q] = dot3((high[rows, :], low[rows, :]), (high[...], low[...]), ((1,), (1,)))
         c = halve(q, 0)
         c.start()
         sent.append(c)
@@ -251,49 +258,83 @@
     for s in (4, 3, 2, 1, 0):
         for q in range(4):
             take(q, s).wait_recv()
+
+    rows, rank = q0_ref.shape
+    tile = 256
+    q_ref[...] = q0_ref[...]
+
+    @pl.loop(0, iters)
+    def _(it):
+        @pl.loop(0, rows // tile)
+        def _(t):
+            at = pl.ds(pl.multiple_of(t * tile, tile), tile)
+            y_ref[at, :] = jnp.dot(out_ref[at, :], q_ref[...], precision=HI, preferred_element_type=jnp.float32)
+
+        q_ref[...] = y_ref[...]
+
+        @pl.loop(0, 2)
+        def _(twice):
+            mapped = q_ref[...]
+            a_ref[...] = lax.dot_general(mapped, mapped, (((0,), (0,)), ((), ())), precision=HI,
+                                         preferred_element_type=jnp.float32)
+            inverse_factor(a_ref, rank)
+            q_ref[...] = lax.dot_general(q_ref[...], a_ref[...], (((1,), (1,)), ((), ())), precision=HI,
+                                         preferred_element_type=jnp.float32)
+
+    basis = split(q_ref[...])
+    made = dot3(basis, (high[...], low[...]), ((0,), (0,)))
+    share = rank // 4
+    width = 128
+    for t in range(4):
+        proj[t, :, pl.ds(pl.multiple_of(core * width, width), width)] = made[t * share:(t + 1) * share, 0:width]
+        proj[t, :, pl.ds(pl.multiple_of((1 - core) * width, width), width)] = made[t * share:(t + 1) * share, width:]
+    zl = z % 2
+    span = pl.ds(pl.multiple_of(zl * 2 * width, 2 * width), 2 * width)
+    c = remote(proj.at[(1 - zl) * 2 + core], core_ref.at[:, span], last_sems.at[0], last_sems.at[1],
+               device_at(x, y, z + 1 - 2 * zl, core))
+    c.start()
+    core_ref[:, span] = proj[gy]
+    index = (gx * 4 + gy) * 4 + sa
+    block = q_ref[pl.ds(pl.multiple_of((index // 2) * 8, 8), 8), :]
+    flag = jnp.broadcast_to(index % 2, (4, rank))
+    rows_ref[...] = jnp.where(flag == 0, block[0:4, :], block[4:8, :])
+    c.wait_recv()
+    sent.append(c)
     for c in sent:
         c.wait_send()
 
-def summed_gram(fibre, scale):
-    nx, width = fibre.shape
+
+def whole(field, start, scale, iters):
+    species, nx, width = field.shape[0], start.shape[0], field.shape[2]
+    rank = start.shape[1]
     dma = lambda *shape: pltpu.SemaphoreType.DMA(shape)
     vm = lambda *shape: pltpu.VMEM(shape, jnp.float32)
+    half = lambda *shape: pltpu.VMEM(shape, jnp.bfloat16)
     return pl.pallas_call(
-        functools.partial(gram_body, scale),
-        out_shape=jax.ShapeDtypeStruct((nx, nx), jnp.float32),
-        in_specs=[pl.BlockSpec(memory_space=pltpu.VMEM)],
-        out_specs=pl.BlockSpec(memory_space=pltpu.VMEM),
+        functools.partial(whole_body, scale, iters),
+        out_shape=(jax.ShapeDtypeStruct((rank // 4, 4 * width), jnp.float32),
+                   jax.ShapeDtypeStruct((nx // 256, rank), jnp.float32)),
+        in_specs=[pl.BlockSpec(memory_space=pltpu.VMEM)] * 2,
+        out_specs=(pl.BlockSpec(memory_space=pltpu.VMEM),) * 2,
         scratch_shapes=[
-            vm(nx, 2 * width), vm(4, 128, nx),
+            vm(16, 64, width), vm(16, 64, width), half(nx, 2 * width), half(nx, 2 * width), vm(4, 128, nx),
             vm(4, 64, nx), vm(4, 32, nx), vm(4, 16, nx), vm(4, 8, nx),
-            vm(8, 4, 8, 128), vm(7, 4, 8, 128), vm(8, 4, 8, 128),
-            dma(2), dma(4, 4), dma(4, 4), dma(7), dma(7), dma(7), dma(7),
-            dma(4, 4), dma(4, 4), dma(5, 4), dma(5, 4),
+            vm(8, 4, 8, 128), vm(7, 4, 8, 128), vm(8, 4, 8, 128), vm(nx, nx),
+            vm(nx, rank), vm(nx, rank), vm(rank, rank), vm(4, rank // 4, 2 * width),
+            dma(15), dma(15), dma(16), dma(16), dma(4, 4), dma(4, 4), dma(7), dma(7), dma(7), dma(7),
+            dma(4, 4), dma(4, 4), dma(5, 4), dma(5, 4), dma(2),
         ],
         compiler_params=pltpu.CompilerParams(collective_id=0, has_side_effects=True,
-                                             vmem_limit_bytes=40 * 1024 * 1024),
-        name="summed_gram",
-    )(fibre)
+                                             vmem_limit_bytes=48 * 1024 * 1024),
+        name="whole",
+    )(field, start)
 
 
 def on_device(scalar_field, start_basis):
-    fibres = lax.all_to_all(scalar_field, "gx", split_axis=0, concat_axis=2, tiled=True)
-    total_cols = fibres.shape[3] * lax.axis_size("gy") * S * fibres.shape[1]
-    devices = lax.axis_size(("gx", "gy", "sa"))
-    rows_dev = NX // devices
-    my_index = lax.axis_index(("gx", "gy", "sa"))
-    gram_matrix = summed_gram(fibres.reshape(NX, fibres.shape[3]), 1.0 / total_cols)
-    cur_basis = iterate(gram_matrix, start_basis, ITERS)
-    own_rows = lax.dynamic_slice_in_dim(cur_basis, my_index * rows_dev, rows_dev, 0)
-    projected = jnp.einsum(
-        "xk,stxy->stky",
-        cur_basis,
-        fibres,
-        precision=HIGHEST_PREC,
-        preferred_element_type=jnp.float32,
-    )
-    core_tensor = lax.all_to_all(projected, "gy", split_axis=2, concat_axis=3, tiled=True)
-    return (core_tensor, own_rows)
+    species, steps, rows, width = scalar_field.shape
+    total_cols = width * lax.axis_size("gy") * S * steps
+    core_tensor, own_rows = whole(scalar_field.reshape(species, rows, width), start_basis, 1.0 / total_cols, ITERS)
+    return (core_tensor.reshape(1, steps, *core_tensor.shape), own_rows)
 
 
 def solution(mesh):

time: 149 us -> 136 us (0.913)
  Pallas kernels: 111 us -> 132 us
  waiting for transfers between devices: 18.9 us -> 0 us
  starting transfers between devices: 15 us -> 0 us
  local copies, waits for them, and re-layouts: 1.22 us -> 3.29 us
  matrix products: 1.63 us -> 0 us
    pallas_call x2 -> x1, Pallas kernels: 111 us -> 132 us  [whole(): pl.pallas_call(functools.partial(whole_body, scale, iters), out_shape=(ja...]
    all_to_all x2 -> x0, waiting for transfers between devices: 18.9 us -> none  [the longest x1 16.3 us: on_device(): lax.all_to_all(scalar_field, 'gx', split_axis=0, concat_axis=2, tiled=True)]
    all_to_all x2 -> x0, starting transfers between devices: 15 us -> none  [the longest x1 11.7 us: on_device(): lax.all_to_all(scalar_field, 'gx', split_axis=0, concat_axis=2, tiled=True)]
    unnamed x2 -> x6, local copies, waits for them, and re-layouts: 0.01 us -> 3.29 us
    dot_general x1 -> x0, matrix products: 1.63 us -> none  [on_device(): jnp.einsum('xk,stxy->stky', cur_basis, fibres, precision=HIGHEST_PREC, pr...]
  transfers between devices with their start and end apart: 2 -> 0, of which waited for: 2 -> 0; matrix products, arithmetic and copies ran while one was open for 0% -> 0% of each run, Pallas kernels for 0% -> 0%
where the time goes in v3:
time: 136 us
  Pallas kernels  132 us (97%)
  local copies, waits for them, and re-layouts  3.29 us (2%)
    pallas_call x1, Pallas kernels, whole(): pl.pallas_call(functools.partial(whole_body, scale, iters), out_shape=(ja...  132 us
    unnamed x6, local copies, waits for them, and re-layouts  3.29 us

profile of v3, /device:TPU:1, one launch (start us, length us, event | category | flops | bytes accessed | tf_op | source)
XLA Modules:
  0.0 135.8 jit_solution(9159732464319415288)
XLA Ops:
  0.6 0.0 copy-start
  0.6 1.0 copy-done
  1.7 0.0 copy-start.1
  1.7 1.0 copy-done.1
  2.7 131.9 %whole.1 = (f32[32,512]{1,0:T(8,128)S(1)}, f32[4,128]{1,0:T(4,128)S(1)}) custom-call(f32[16,64,128]{2,1,0:T(8,128)S(1)} %bitcast.2, f32[1024,128]{1,0:T(8,128)S(1)} %copy-done.1), custom_call_target="tpu_custom_call" | custom-call | tf_op jit(solution)/shard_map/whole/pallas_call | solution.py:313
  134.6 0.6 copy.6
  135.2 0.6 copy.7
Async XLA Ops:
  0.6 1.0 copy-start
  1.7 1.0 copy-start.1

commit v4 on v3

--- a/solution.py
+++ b/solution.py
@@ -81,13 +81,20 @@
     return high, (v - high.astype(jnp.float32)).astype(jnp.bfloat16)
 
 
+def thirds(v):
+    big, rest = v.astype(jnp.bfloat16), v
+    rest = rest - big.astype(jnp.float32)
+    mid = rest.astype(jnp.bfloat16)
+    return big, mid, (rest - mid.astype(jnp.float32)).astype(jnp.bfloat16)
+
+
 def dot3(a, b, contract):
     one = lambda u, v: lax.dot_general(u, v, (contract, ((), ())), preferred_element_type=jnp.float32)
     return one(a[0], b[0]) + (one(a[0], b[1]) + one(a[1], b[0]))
 
 
 def whole_body(scale, iters, field_ref, q0_ref, core_ref, rows_ref, own, other, high, low, part, r0, r1, r2, r3,
-               zout, zin, zall, out_ref, q_ref, y_ref, a_ref, proj,
+               zout, zin, zall, gsym, gram, parts_q, q_ref, a_ref, proj,
                fs_send, fs_recv, fw_send, fw_recv, rs_send, rs_recv, zr_send, zr_recv, za_send, za_recv,
                ag_send, ag_recv, core_send, core_recv, last_sems):
     x, y, z, core = place()
@@ -133,8 +140,10 @@
     sent.append(c)
 
     def store(block, values, lanes):
-        rows = pl.ds(pl.multiple_of(block * 64, 64), 64)
-        high[rows, lanes], low[rows, lanes] = split(values)
+        halves = split(values)
+        for first in (0, 1024):
+            rows = pl.ds(pl.multiple_of(block * 64 + first, 64), 64)
+            high[rows, lanes], low[rows, lanes] = halves
 
     mine, its = slice(0, 128), slice(128, 256)
     store(gx, field_ref[gx], mine)
@@ -168,7 +177,8 @@
     top = core * 512
     for q in range(4):
         rows = pl.ds(pl.multiple_of(top + q * 128, 128), 128)
-        part[q] = dot3((high[rows, :], low[rows, :]), (high[...], low[...]), ((1,), (1,)))
+        window = pl.ds(pl.multiple_of(top + q * 128, 128), 640)
+        part[q] = dot3((high[rows, :], low[rows, :]), (high[window, :], low[window, :]), ((1,), (1,)))
         c = halve(q, 0)
         c.start()
         sent.append(c)
@@ -182,10 +192,13 @@
                 c = halve(q, s + 1)
                 c.start()
                 sent.append(c)
-    for q in range(4):
-        rows = pl.ds(pl.multiple_of(offs[q][4], 8), 8)
-        for t in range(8):
-            zout[t, q] = part[q, rows, 128 * t:128 * t + 128]
+    for n in range(24):
+        q, lanes = n // 5, slice(128 * (n % 5), 128 * (n % 5) + 128)
+        if n < 20:
+            zout[n % 8, n // 8] = part[q, pl.ds(pl.multiple_of(offs[q][4], 8), 8), lanes]
+        else:
+            zout[n % 8, n // 8] = jnp.zeros((8, 128), jnp.float32)
+
     def zscatter(o):
         return remote(zout.at[(z + o) % 8], zin.at[o - 1], zr_send.at[o - 1], zr_recv.at[o - 1], zpeers[o - 1])
     def zgather(o):
@@ -207,15 +220,14 @@
     def at_row(q, row, size):
         return pl.ds(pl.multiple_of(top + q * 128 + row, 8), size)
 
-    for o in range(8):
-        if o:
-            zgather(o).wait_recv()
-        lanes = pl.ds(pl.multiple_of(((z + 8 - o) % 8) * 128, 128), 128)
-        for q in range(4):
-            out_ref[at_row(q, offs[q][4], 8), lanes] = zall[o, q]
+    for o in range(1, 8):
+        zgather(o).wait_recv()
+    for n in range(20):
+        q, lanes = n // 5, slice(128 * (n % 5), 128 * (n % 5) + 128)
+        gsym[at_row(q, offs[q][4], 8), lanes] = zall[(z + 8 - n % 8) % 8, n // 8]
 
     def grow(q, s):
-        ref = out_ref.at[at_row(q, offs[q][s + 1], 64 >> s), :]
+        ref = gsym.at[at_row(q, offs[q][s + 1], 64 >> s), :]
         return remote(ref, ref, ag_send.at[s, q], ag_recv.at[s, q], dims[(q + s) % 4][1])
 
     def hand(q, s):
@@ -224,7 +236,7 @@
         else:
             half = 64 >> s
             rows = at_row(q, offs[q][s] + (1 - dims[(q + s) % 4][0]) * half, half)
-        ref = out_ref.at[rows, :]
+        ref = gsym.at[rows, :]
         return remote(ref, ref, core_send.at[s, q], core_recv.at[s, q], mate)
 
     def take(q, s):
@@ -233,14 +245,14 @@
         else:
             size = 64 >> s
             row = offs[q][s] + (1 - dims[(q + s) % 4][0]) * size
-        ref = out_ref.at[pl.ds(pl.multiple_of(512 - top + q * 128 + row, 8), size), :]
+        ref = gsym.at[pl.ds(pl.multiple_of(512 - top + q * 128 + row, 8), size), :]
         return remote(ref, ref, core_send.at[s, q], core_recv.at[s, q], mate)
 
     for s in (3, 2, 1, 0):
         for q in range(4):
             if s < 3:
                 grown = offs[q][s + 1] + (1 - dims[(q + s + 1) % 4][0]) * (64 >> (s + 1))
-                ref = out_ref.at[at_row(q, grown, 64 >> (s + 1)), :]
+                ref = gsym.at[at_row(q, grown, 64 >> (s + 1)), :]
                 remote(ref, ref, ag_send.at[s + 1, q], ag_recv.at[s + 1, q], mate).wait_recv()
             c = grow(q, s)
             c.start()
@@ -250,7 +262,7 @@
             sent.append(c)
     for q in range(4):
         grown = offs[q][0] + (1 - dims[q % 4][0]) * 64
-        ref = out_ref.at[at_row(q, grown, 64), :]
+        ref = gsym.at[at_row(q, grown, 64), :]
         remote(ref, ref, ag_send.at[0, q], ag_recv.at[0, q], mate).wait_recv()
         c = hand(q, 0)
         c.start()
@@ -262,15 +274,31 @@
     rows, rank = q0_ref.shape
     tile = 256
     q_ref[...] = q0_ref[...]
+    for i in range(8):
+        for b in range(5):
+            j = (i + b) % 8
+            block = gsym[128 * i:128 * i + 128, 128 * b:128 * b + 128]
+            spots = [(i, j, block)]
+            if 0 < b < 4:
+                spots.append((j, i, block.T))
+            for row, col, value in spots:
+                for n, piece in enumerate(thirds(value)):
+                    gram[n, 128 * row:128 * row + 128, 128 * col:128 * col + 128] = piece
 
     @pl.loop(0, iters)
     def _(it):
+        for n, piece in enumerate(thirds(q_ref[...])):
+            parts_q[:, 128 * n:128 * n + 128] = piece
+
         @pl.loop(0, rows // tile)
         def _(t):
             at = pl.ds(pl.multiple_of(t * tile, tile), tile)
-            y_ref[at, :] = jnp.dot(out_ref[at, :], q_ref[...], precision=HI, preferred_element_type=jnp.float32)
-
-        q_ref[...] = y_ref[...]
+            one = lambda u, v: jnp.dot(u, v, preferred_element_type=jnp.float32)
+            big, mid, small = gram[0, at, :], gram[1, at, :], gram[2, at, :]
+            both = parts_q[:, 0:256]
+            wide = one(big, both) + one(mid, both)
+            tiny = one(big, parts_q[:, 256:384]) + one(small, parts_q[:, 0:128])
+            q_ref[at, :] = wide[:, 0:128] + (wide[:, 128:256] + tiny)
 
         @pl.loop(0, 2)
         def _(twice):
@@ -282,7 +310,7 @@
                                          preferred_element_type=jnp.float32)
 
     basis = split(q_ref[...])
-    made = dot3(basis, (high[...], low[...]), ((0,), (0,)))
+    made = dot3(basis, (high[0:rows, :], low[0:rows, :]), ((0,), (0,)))
     share = rank // 4
     width = 128
     for t in range(4):
@@ -317,10 +345,10 @@
         in_specs=[pl.BlockSpec(memory_space=pltpu.VMEM)] * 2,
         out_specs=(pl.BlockSpec(memory_space=pltpu.VMEM),) * 2,
         scratch_shapes=[
-            vm(16, 64, width), vm(16, 64, width), half(nx, 2 * width), half(nx, 2 * width), vm(4, 128, nx),
-            vm(4, 64, nx), vm(4, 32, nx), vm(4, 16, nx), vm(4, 8, nx),
-            vm(8, 4, 8, 128), vm(7, 4, 8, 128), vm(8, 4, 8, 128), vm(nx, nx),
-            vm(nx, rank), vm(nx, rank), vm(rank, rank), vm(4, rank // 4, 2 * width),
+            vm(16, 64, width), vm(16, 64, width), half(2 * nx, 2 * width), half(2 * nx, 2 * width),
+            vm(4, 128, 640), vm(4, 64, 640), vm(4, 32, 640), vm(4, 16, 640), vm(4, 8, 640),
+            vm(8, 3, 8, 128), vm(7, 3, 8, 128), vm(8, 3, 8, 128), vm(nx, 640),
+            half(3, nx, nx), half(nx, 3 * rank), vm(nx, rank), vm(rank, rank), vm(4, rank // 4, 2 * width),
             dma(15), dma(15), dma(16), dma(16), dma(4, 4), dma(4, 4), dma(7), dma(7), dma(7), dma(7),
             dma(4, 4), dma(4, 4), dma(5, 4), dma(5, 4), dma(2),
         ],

time: 136 us -> 127 us (0.934)
  Pallas kernels: 132 us -> 122 us
    pallas_call x1, Pallas kernels: 132 us -> 122 us  [whole(): pl.pallas_call(functools.partial(whole_body, scale, iters), out_shape=(ja...]
where the time goes in v4:
time: 127 us; the launch traced here: 126 us
  Pallas kernels  122 us (96%)
  local copies, waits for them, and re-layouts  3.29 us (3%)
    pallas_call x1, Pallas kernels, whole(): pl.pallas_call(functools.partial(whole_body, scale, iters), out_shape=(ja...  122 us
    unnamed x6, local copies, waits for them, and re-layouts  3.29 us

profile of v4, /device:TPU:1, one launch (start us, length us, event | category | flops | bytes accessed | tf_op | source)
XLA Modules:
  0.0 126.4 jit_solution(15977227719878781575)
XLA Ops:
  0.6 0.0 copy-start
  0.6 1.0 copy-done
  1.7 0.0 copy-start.1
  1.7 1.0 copy-done.1
  2.7 122.4 %whole.1 = (f32[32,512]{1,0:T(8,128)S(1)}, f32[4,128]{1,0:T(4,128)S(1)}) custom-call(f32[16,64,128]{2,1,0:T(8,128)S(1)} %bitcast.2, f32[1024,128]{1,0:T(8,128)S(1)} %copy-done.1), custom_call_target="tpu_custom_call" | custom-call | tf_op jit(solution)/shard_map/whole/pallas_call | solution.py:341
  125.2 0.6 copy.6
  125.8 0.6 copy.7
Async XLA Ops:
  0.6 1.0 copy-start
  1.7 1.0 copy-start.1

commit v5 on v4

--- a/solution.py
+++ b/solution.py
@@ -11,7 +11,7 @@
 S = 64
 ITERS = 3
 
-HI = lax.Precision.HIGHEST
+TOP = float(jnp.finfo(jnp.float32).max)
 MESH = pl.DeviceIdType.MESH
 
 def place():
@@ -26,7 +26,7 @@
     return jnp.broadcast_to(v[p:p + 1, :], v.shape)
 
 def lane_of(v, c):
-    return jnp.broadcast_to(v[:, c:c + 1], v.shape)
+    return jnp.minimum(jnp.broadcast_to(v[:, c:c + 1], v.shape), TOP)
 
 def inverse_factor(a_ref, rank):
     sub = lax.broadcasted_iota(jnp.int32, (8, rank), 0)
@@ -68,8 +68,10 @@
         if k + 2 < panels:
             low = base + 16
             upper = jnp.where(lane >= low, scaled, 0.0)
-            upd = lax.dot_general(upper, scaled, (((0,), (0,)), ((), ())), precision=HI,
-                                  preferred_element_type=jnp.float32)
+            left, right = thirds(upper), thirds(scaled)
+            pick = lambda v, order: jnp.concatenate([v[n].astype(jnp.float32) for n in order]).astype(jnp.bfloat16)
+            upd = lax.dot_general(pick(left, (0, 0, 1, 1, 0, 2)), pick(right, (0, 1, 0, 1, 2, 0)),
+                                  (((0,), (0,)), ((), ())), preferred_element_type=jnp.float32)
             rest = a_ref[low:, :]
             lanes = lax.broadcasted_iota(jnp.int32, rest.shape, 1)
             rest = jnp.where((lanes >= base) & (lanes < base + 8), 0.0, rest)
@@ -273,7 +275,13 @@
 
     rows, rank = q0_ref.shape
     tile = 256
-    q_ref[...] = q0_ref[...]
+    one = lambda u, v: jnp.dot(u, v, preferred_element_type=jnp.float32)
+
+    def keep(at, values):
+        for n, piece in enumerate(thirds(values)):
+            parts_q[at, 128 * n:128 * n + 128] = piece
+
+    keep(slice(0, rows), q0_ref[...])
     for i in range(8):
         for b in range(5):
             j = (i + b) % 8
@@ -287,29 +295,33 @@
 
     @pl.loop(0, iters)
     def _(it):
-        for n, piece in enumerate(thirds(q_ref[...])):
-            parts_q[:, 128 * n:128 * n + 128] = piece
-
         @pl.loop(0, rows // tile)
         def _(t):
             at = pl.ds(pl.multiple_of(t * tile, tile), tile)
-            one = lambda u, v: jnp.dot(u, v, preferred_element_type=jnp.float32)
             big, mid, small = gram[0, at, :], gram[1, at, :], gram[2, at, :]
             both = parts_q[:, 0:256]
             wide = one(big, both) + one(mid, both)
             tiny = one(big, parts_q[:, 256:384]) + one(small, parts_q[:, 0:128])
             q_ref[at, :] = wide[:, 0:128] + (wide[:, 128:256] + tiny)
 
+        keep(slice(0, rows), q_ref[...])
+
         @pl.loop(0, 2)
         def _(twice):
-            mapped = q_ref[...]
-            a_ref[...] = lax.dot_general(mapped, mapped, (((0,), (0,)), ((), ())), precision=HI,
-                                         preferred_element_type=jnp.float32)
+            inner = lambda u, v: lax.dot_general(u, v, (((0,), (0,)), ((), ())), preferred_element_type=jnp.float32)
+            both = parts_q[:, 0:256]
+            four = inner(both, both)
+            cross = inner(parts_q[:, 0:128], parts_q[:, 256:384]) + four[0:128, 128:256]
+            a_ref[...] = four[0:128, 0:128] + ((cross + cross.T) + four[128:256, 128:256])
             inverse_factor(a_ref, rank)
-            q_ref[...] = lax.dot_general(q_ref[...], a_ref[...], (((1,), (1,)), ((), ())), precision=HI,
-                                         preferred_element_type=jnp.float32)
-
-    basis = split(q_ref[...])
+            f_big, f_mid, f_small = thirds(a_ref[...].T)
+            main = jnp.concatenate([jnp.concatenate([f_big, f_big]), jnp.concatenate([f_mid, f_mid])], axis=1)
+            wide = one(parts_q[:, 0:256], main)
+            tiny = one(parts_q[:, 0:128], f_small) + one(parts_q[:, 256:384], f_big)
+            q_ref[...] = wide[:, 0:128] + (wide[:, 128:256] + tiny)
+            keep(slice(0, rows), q_ref[...])
+
+    basis = (parts_q[:, 0:128], parts_q[:, 128:256])
     made = dot3(basis, (high[0:rows, :], low[0:rows, :]), ((0,), (0,)))
     share = rank // 4
     width = 128

time: 127 us -> 118 us (0.929)
  Pallas kernels: 122 us -> 114 us
    pallas_call x1, Pallas kernels: 122 us -> 114 us  [whole(): pl.pallas_call(functools.partial(whole_body, scale, iters), out_shape=(ja...]
where the time goes in v5:
time: 118 us
  Pallas kernels  114 us (97%)
  local copies, waits for them, and re-layouts  3.29 us (3%)
    pallas_call x1, Pallas kernels, whole(): pl.pallas_call(functools.partial(whole_body, scale, iters), out_shape=(ja...  114 us
    unnamed x6, local copies, waits for them, and re-layouts  3.29 us

profile of v5, /device:TPU:1, one launch (start us, length us, event | category | flops | bytes accessed | tf_op | source)
XLA Modules:
  0.0 117.8 jit_solution(700974373409290178)
XLA Ops:
  0.6 0.0 copy-start
  0.6 1.0 copy-done
  1.7 0.0 copy-start.1
  1.7 1.0 copy-done.1
  2.7 113.9 %whole.1 = (f32[32,512]{1,0:T(8,128)S(1)}, f32[4,128]{1,0:T(4,128)S(1)}) custom-call(f32[16,64,128]{2,1,0:T(8,128)S(1)} %bitcast.2, f32[1024,128]{1,0:T(8,128)S(1)} %copy-done.1), custom_call_target="tpu_custom_call" | custom-call | tf_op jit(solution)/shard_map/whole/pallas_call | solution.py:353
  116.6 0.6 copy.6
  117.2 0.6 copy.7
Async XLA Ops:
  0.6 1.0 copy-start
  1.7 1.0 copy-start.1

commit v6 on v5

--- a/solution.py
+++ b/solution.py
@@ -98,7 +98,7 @@
 def whole_body(scale, iters, field_ref, q0_ref, core_ref, rows_ref, own, other, high, low, part, r0, r1, r2, r3,
                zout, zin, zall, gsym, gram, parts_q, q_ref, a_ref, proj,
                fs_send, fs_recv, fw_send, fw_recv, rs_send, rs_recv, zr_send, zr_recv, za_send, za_recv,
-               ag_send, ag_recv, core_send, core_recv, last_sems):
+               ag_send, ag_recv, core_send, core_recv, last_sems, local_sems):
     x, y, z, core = place()
     rbufs = (r0, r1, r2, r3)
     mate = device_at(x, y, z, 1 - core)
@@ -111,6 +111,11 @@
     )
     zpeers = [device_at(x, y, (z + o) % 8, core) for o in range(1, 8)]
 
+    load_own = pltpu.make_async_copy(field_ref.at[lax.axis_index("gx")], own.at[lax.axis_index("gx")],
+                                     local_sems.at[0])
+    load_own.start()
+    load_start = pltpu.make_async_copy(q0_ref, q_ref, local_sems.at[1])
+    load_start.start()
     barrier = pltpu.get_barrier_semaphore()
     gx, gy, sa = lax.axis_index("gx"), lax.axis_index("gy"), lax.axis_index("sa")
     xpeers = [{"gx": (gx + o) % 16, "gy": gy, "sa": sa} for o in range(1, 16)]
@@ -129,14 +134,14 @@
 
     def forward(o):
         block = (gx + 16 - o) % 16
-        src = own.at[block] if o else field_ref.at[block]
-        return remote(src, other.at[block], fw_send.at[o], fw_recv.at[o], mate)
+        return remote(own.at[block], other.at[block], fw_send.at[o], fw_recv.at[o], mate)
 
     order = (8, 4, 12, 6, 10, 7, 9, 5, 11, 2, 14, 3, 13, 1, 15)
     for o in order:
         c = spread(o)
         c.start()
         sent.append(c)
+    load_own.wait()
     c = forward(0)
     c.start()
     sent.append(c)
@@ -148,7 +153,7 @@
             high[rows, lanes], low[rows, lanes] = halves
 
     mine, its = slice(0, 128), slice(128, 256)
-    store(gx, field_ref[gx], mine)
+    store(gx, own[gx], mine)
     for o in reversed(order):
         block = (gx + 16 - o) % 16
         spread(o).wait_recv()
@@ -158,7 +163,7 @@
         store(block, own[block], mine)
     for o in (0,) + order[::-1]:
         block = (gx + 16 - o) % 16
-        remote(field_ref.at[0], other.at[block], fw_send.at[o], fw_recv.at[o], mate).wait_recv()
+        remote(own.at[0], other.at[block], fw_send.at[o], fw_recv.at[o], mate).wait_recv()
         store(block, other[block], its)
 
     offs = []
@@ -262,6 +267,18 @@
             c = hand(q, s + 1)
             c.start()
             sent.append(c)
+    def unpack(i):
+        for b in range(5):
+            j = (i + b) % 8
+            block = gsym[pl.ds(pl.multiple_of(128 * i, 128), 128), 128 * b:128 * b + 128]
+            spots = [(i, j, block)]
+            if 0 < b < 4:
+                spots.append((j, i, block.T))
+            for row, col, value in spots:
+                for n, piece in enumerate(thirds(value)):
+                    gram[n, pl.ds(pl.multiple_of(128 * row, 128), 128),
+                         pl.ds(pl.multiple_of(128 * col, 128), 128)] = piece
+
     for q in range(4):
         grown = offs[q][0] + (1 - dims[q % 4][0]) * 64
         ref = gsym.at[at_row(q, grown, 64), :]
@@ -269,9 +286,11 @@
         c = hand(q, 0)
         c.start()
         sent.append(c)
-    for s in (4, 3, 2, 1, 0):
-        for q in range(4):
+        unpack(core * 4 + q)
+    for q in range(4):
+        for s in (4, 3, 2, 1, 0):
             take(q, s).wait_recv()
+        unpack((1 - core) * 4 + q)
 
     rows, rank = q0_ref.shape
     tile = 256
@@ -281,17 +300,8 @@
         for n, piece in enumerate(thirds(values)):
             parts_q[at, 128 * n:128 * n + 128] = piece
 
-    keep(slice(0, rows), q0_ref[...])
-    for i in range(8):
-        for b in range(5):
-            j = (i + b) % 8
-            block = gsym[128 * i:128 * i + 128, 128 * b:128 * b + 128]
-            spots = [(i, j, block)]
-            if 0 < b < 4:
-                spots.append((j, i, block.T))
-            for row, col, value in spots:
-                for n, piece in enumerate(thirds(value)):
-                    gram[n, 128 * row:128 * row + 128, 128 * col:128 * col + 128] = piece
+    load_start.wait()
+    keep(slice(0, rows), q_ref[...])
 
     @pl.loop(0, iters)
     def _(it):
@@ -354,7 +364,7 @@
         functools.partial(whole_body, scale, iters),
         out_shape=(jax.ShapeDtypeStruct((rank // 4, 4 * width), jnp.float32),
                    jax.ShapeDtypeStruct((nx // 256, rank), jnp.float32)),
-        in_specs=[pl.BlockSpec(memory_space=pltpu.VMEM)] * 2,
+        in_specs=[pl.BlockSpec(memory_space=pltpu.HBM)] * 2,
         out_specs=(pl.BlockSpec(memory_space=pltpu.VMEM),) * 2,
         scratch_shapes=[
             vm(16, 64, width), vm(16, 64, width), half(2 * nx, 2 * width), half(2 * nx, 2 * width),
@@ -362,7 +372,7 @@
             vm(8, 3, 8, 128), vm(7, 3, 8, 128), vm(8, 3, 8, 128), vm(nx, 640),
             half(3, nx, nx), half(nx, 3 * rank), vm(nx, rank), vm(rank, rank), vm(4, rank // 4, 2 * width),
             dma(15), dma(15), dma(16), dma(16), dma(4, 4), dma(4, 4), dma(7), dma(7), dma(7), dma(7),
-            dma(4, 4), dma(4, 4), dma(5, 4), dma(5, 4), dma(2),
+            dma(4, 4), dma(4, 4), dma(5, 4), dma(5, 4), dma(2), dma(2),
         ],
         compiler_params=pltpu.CompilerParams(collective_id=0, has_side_effects=True,
                                              vmem_limit_bytes=48 * 1024 * 1024),

time: 118 us -> 117 us (level)
  no operation moved by 1% of the time
where the time goes in v6:
time: 117 us
  Pallas kernels  113 us (97%)
  local copies, waits for them, and re-layouts  3.29 us (3%)
    pallas_call x1, Pallas kernels, whole(): pl.pallas_call(functools.partial(whole_body, scale, iters), out_shape=(ja...  113 us
    unnamed x6, local copies, waits for them, and re-layouts  3.29 us

profile of v6, /device:TPU:1, one launch (start us, length us, event | category | flops | bytes accessed | tf_op | source)
XLA Modules:
  0.0 116.8 jit_solution(10123033711052436764)
XLA Ops:
  0.6 0.0 copy-start
  0.6 1.0 copy-done
  1.7 0.0 copy-start.1
  1.7 1.0 copy-done.1
  2.7 112.9 %whole.1 = (f32[32,512]{1,0:T(8,128)S(1)}, f32[4,128]{1,0:T(4,128)S(1)}) custom-call(f32[16,64,128]{2,1,0:T(8,128)S(1)} %bitcast.2, f32[1024,128]{1,0:T(8,128)S(1)} %copy-done.1), custom_call_target="tpu_custom_call" | custom-call | tf_op jit(solution)/shard_map/whole/pallas_call | solution.py:363
  115.6 0.6 copy.6
  116.2 0.6 copy.7
Async XLA Ops:
  0.6 1.0 copy-start
  1.7 1.0 copy-start.1

commit v7 on v6

--- a/solution.py
+++ b/solution.py
@@ -293,7 +293,7 @@
         unpack((1 - core) * 4 + q)
 
     rows, rank = q0_ref.shape
-    tile = 256
+    tile = 512
     one = lambda u, v: jnp.dot(u, v, preferred_element_type=jnp.float32)
 
     def keep(at, values):

time: 117 us -> 116 us (level)
  no operation moved by 1% of the time
where the time goes in v7:
time: 116 us
  Pallas kernels  112 us (97%)
  local copies, waits for them, and re-layouts  3.29 us (3%)
    pallas_call x1, Pallas kernels, whole(): pl.pallas_call(functools.partial(whole_body, scale, iters), out_shape=(ja...  112 us
    unnamed x6, local copies, waits for them, and re-layouts  3.29 us

profile of v7, /device:TPU:1, one launch (start us, length us, event | category | flops | bytes accessed | tf_op | source)
XLA Modules:
  0.0 115.7 jit_solution(13109380771218215361)
XLA Ops:
  0.6 0.0 copy-start
  0.6 1.0 copy-done
  1.7 0.0 copy-start.1
  1.7 1.0 copy-done.1
  2.7 111.8 %whole.1 = (f32[32,512]{1,0:T(8,128)S(1)}, f32[4,128]{1,0:T(4,128)S(1)}) custom-call(f32[16,64,128]{2,1,0:T(8,128)S(1)} %bitcast.2, f32[1024,128]{1,0:T(8,128)S(1)} %copy-done.1), custom_call_target="tpu_custom_call" | custom-call | tf_op jit(solution)/shard_map/whole/pallas_call | solution.py:363
  114.5 0.6 copy.6
  115.1 0.6 copy.7
Async XLA Ops:
  0.6 1.0 copy-start
  1.7 1.0 copy-start.1
